TPU v7x, 32 devices: a whole 2x2x4 slice. The times are simulated.
32 devices in a mesh: wide: 16 (over z, y, core), narrow: 2 (over x).
Axes of the slice: x: 2, y: 2, z: 4, core: 2. Of those that a mesh axis runs over, the one named last changes fastest.
Arguments:
- frames_in: bfloat16 [32, 256, 1152], P(('wide', 'narrow')), may hold values from -6 to 6
- conditioning: bfloat16 [32, 1152], P(('wide', 'narrow')), may hold values from -5 to 5
- grid: int32 [32, 2], P(('wide', 'narrow')), may hold values from 8 to 32, as said below
- cotangent: bfloat16 [32, 256, 1152], P(('wide', 'narrow')), may hold values from -6 to 6
- mod_weight: float32 [1152, 6912], P(('wide', 'narrow')), may hold values from -0.1875 to 0.1875
- qkv_weight: float32 [1152, 3456], P(('wide', 'narrow')), may hold values from -0.1875 to 0.1875
- out_weight: float32 [1152, 1152], P(('wide', 'narrow')), may hold values from -1 to 1
- up_weight: float32 [1152, 4608], P(('wide', 'narrow')), may hold values from -0.1875 to 0.1875
- down_weight: float32 [4608, 1152], P(('wide', 'narrow')), may hold values from -0.09375 to 0.09375
- biases: float32 [16128], P(('wide', 'narrow')), may hold values from -1.2 to 1.2
- mod_state: float32 [3, 1152, 6912], P(None, ('wide', 'narrow')), as said below
- qkv_state: float32 [3, 1152, 3456], P(None, ('wide', 'narrow')), as said below
- out_state: float32 [3, 1152, 1152], P(None, ('wide', 'narrow')), as said below
- up_state: float32 [3, 1152, 4608], P(None, ('wide', 'narrow')), as said below
- down_state: float32 [3, 4608, 1152], P(None, ('wide', 'narrow')), as said below
- bias_state: float32 [3, 16128], P(None, ('wide', 'narrow')), as said below
Outputs:
- block_out: bfloat16 [32, 256, 1152], P(('wide', 'narrow'))
- frames_grad: bfloat16 [32, 256, 1152], P(('wide', 'narrow'))
- cond_grad: float32 [32, 1152], P(('wide', 'narrow'))
- grad_norm: float32 [], replicated
- mod_grad: float32 [1152, 6912], P(('wide', 'narrow'))
- qkv_grad: float32 [1152, 3456], P(('wide', 'narrow'))
- out_grad: float32 [1152, 1152], P(('wide', 'narrow'))
- up_grad: float32 [1152, 4608], P(('wide', 'narrow'))
- down_grad: float32 [4608, 1152], P(('wide', 'narrow'))
- bias_grad: float32 [16128], P(('wide', 'narrow'))
- mod_new: float32 [1152, 6912], P(('wide', 'narrow'))
- qkv_new: float32 [1152, 3456], P(('wide', 'narrow'))
- out_new: float32 [1152, 1152], P(('wide', 'narrow'))
- up_new: float32 [1152, 4608], P(('wide', 'narrow'))
- down_new: float32 [4608, 1152], P(('wide', 'narrow'))
- bias_new: float32 [16128], P(('wide', 'narrow'))
- mod_state_new: float32 [3, 1152, 6912], P(None, ('wide', 'narrow'))
- qkv_state_new: float32 [3, 1152, 3456], P(None, ('wide', 'narrow'))
- out_state_new: float32 [3, 1152, 1152], P(None, ('wide', 'narrow'))
- up_state_new: float32 [3, 1152, 4608], P(None, ('wide', 'narrow'))
- down_state_new: float32 [3, 4608, 1152], P(None, ('wide', 'narrow'))
- bias_state_new: float32 [3, 16128], P(None, ('wide', 'narrow'))
Inputs may be any that keep to these rules, and one draw needn't show every extreme that they name: Each frame's grid is (16, 16), (12, 20) or (8, 32); frame 0 has the first and frame 1 the last. `mod_state`: slot 0 holds first moments, slot 1 second moments (positive), slot 2 the weight average. `qkv_state`: slot 0 holds first moments, slot 1 second moments (positive), slot 2 the weight average. `out_state`: slot 0 holds first moments, slot 1 second moments (positive), slot 2 the weight average. `up_state`: slot 0 holds first moments, slot 1 second moments (positive), slot 2 the weight average. `down_state`: slot 0 holds first moments, slot 1 second moments (positive), slot 2 the weight average. `bias_state`: slot 0 holds first moments, slot 1 second moments (positive), slot 2 the weight average.
All inputs are finite; a program needn't handle non-finite values.
Results may differ from a plain program's by a relative error of at most 0.014.
The roundings to bfloat16 on the way count: a program that leaves them out, or rounds other values in their place, can miss the bound.
Values may be sent and summed in bfloat16 or wider, within the bound.
A program may use at most 384 MiB of HBM per device.

v0:
```python
import jax
import jax.numpy as jnp
from jax import lax
from jax.sharding import PartitionSpec as P

HEADS = 16
STEPS = 4
CLIP = 576


NORM_EPS = 1e-06
RATE = 0.04
FIRST_DECAY = 0.5
SECOND_DECAY = 0.5
WEIGHT_DECAY = 0.1
ADAM_EPS = 1e-08
AVERAGE_DECAY = 0.9999
MASK_VALUE = -1e30


def layer_norm(values):
    centre = jnp.mean(values, axis=-1, keepdims=True)
    centred = values - centre
    spread = jnp.mean(centred * centred, axis=-1, keepdims=True)
    return centred * lax.rsqrt(spread + NORM_EPS)


def modulate(values, shift_part, scale_part):
    return layer_norm(values) * (1.0 + scale_part) + shift_part


def silu_act(values):
    return values * jax.nn.sigmoid(values)


def gelu_tanh(values):
    inner = 0.7978845608028654 * (values + 0.044715 * values * values * values)
    return 0.5 * values * (1.0 + jnp.tanh(inner))


def slot_mask(grid, frame_len):
    area = grid[:, 0] * grid[:, 1]
    return lax.broadcasted_iota(jnp.int32, (grid.shape[0], frame_len), 1) < area[:, None]


def split_biases(biases, model_width, hidden_width):
    edges = [
        6 * model_width,
        7 * model_width,
        8 * model_width,
        9 * model_width,
        9 * model_width + hidden_width,
    ]
    return jnp.split(biases, edges)


def adam_update(weight, state, grad):
    first = FIRST_DECAY * state[0] + (1.0 - FIRST_DECAY) * grad
    second = SECOND_DECAY * state[1] + (1.0 - SECOND_DECAY) * grad * grad
    first_hat = first / (1.0 - FIRST_DECAY**STEPS)
    second_hat = second / (1.0 - SECOND_DECAY**STEPS)
    new_weight = weight - RATE * (
        first_hat / (jnp.sqrt(second_hat) + ADAM_EPS) + WEIGHT_DECAY * weight
    )
    average = AVERAGE_DECAY * state[2] + (1.0 - AVERAGE_DECAY) * new_weight
    return (new_weight, jnp.stack([first, second, average]))


def attention_scores(query_heads, key_heads, valid_slots, score_scale):
    scores = (
        jnp.einsum("fqhs,fkhs->fhqk", query_heads, key_heads, preferred_element_type=jnp.float32)
        * score_scale
    )
    return jnp.where(valid_slots[:, None, None, :], scores, MASK_VALUE)


def token_sum(values):
    return jnp.sum(values, axis=(0, 1), dtype=jnp.float32)


def owner_split(member, count):
    rows = member.shape[0] // count
    return member.reshape((count, rows) + member.shape[1:])


def source_sum(member, axis_index):
    return jnp.sum(member, axis=axis_index)


def shards(
    frames_in,
    conditioning,
    grid,
    cotangent,
    mod_weight,
    qkv_weight,
    out_weight,
    up_weight,
    down_weight,
    biases,
    mod_state,
    qkv_state,
    out_state,
    up_state,
    down_state,
    bias_state,
):
    frame_count, frame_len, model_width = frames_in.shape
    hidden_width = up_weight.shape[1]
    head_size = model_width // HEADS
    score_scale = head_size ** (-0.5)
    head_shape = (frame_count, frame_len, HEADS, head_size)
    owner_count = lax.axis_size("wide") * lax.axis_size("narrow")
    gathered = (
        lax.all_gather(mod_weight.astype(jnp.bfloat16), ("wide", "narrow"), axis=0, tiled=True),
        lax.all_gather(qkv_weight.astype(jnp.bfloat16), ("wide", "narrow"), axis=0, tiled=True),
        lax.all_gather(out_weight.astype(jnp.bfloat16), ("wide", "narrow"), axis=0, tiled=True),
        lax.all_gather(up_weight.astype(jnp.bfloat16), ("wide", "narrow"), axis=0, tiled=True),
        lax.all_gather(down_weight.astype(jnp.bfloat16), ("wide", "narrow"), axis=0, tiled=True),
        lax.all_gather(biases.astype(jnp.bfloat16), ("wide", "narrow"), axis=0, tiled=True),
    )
    mod_low, qkv_low, out_low, up_low, down_low, bias_low = gathered
    mod_bias, query_bias, value_bias, out_bias, up_bias, down_bias = split_biases(
        bias_low.astype(jnp.float32), model_width, hidden_width
    )
    valid_slots = slot_mask(grid, frame_len)
    row_mask = valid_slots[:, :, None].astype(jnp.float32)
    frames_f = frames_in.astype(jnp.float32)
    cond_f = conditioning.astype(jnp.float32)
    silu_low = silu_act(cond_f).astype(jnp.bfloat16)
    modulation = jnp.dot(silu_low, mod_low, preferred_element_type=jnp.float32) + mod_bias
    shift_attn, scale_attn, gate_attn, shift_mlp, scale_mlp, gate_mlp = jnp.split(
        modulation[:, None, :], 6, axis=-1
    )
    norm_one = modulate(frames_f, shift_attn, scale_attn).astype(jnp.bfloat16)
    qkv_bias = jnp.concatenate([query_bias, jnp.zeros_like(query_bias), value_bias])
    qkv_vals = (
        jnp.einsum("fbd,de->fbe", norm_one, qkv_low, preferred_element_type=jnp.float32) + qkv_bias
    ).astype(jnp.bfloat16)
    query_heads = qkv_vals[:, :, :model_width].reshape(head_shape)
    key_heads = qkv_vals[:, :, model_width : 2 * model_width].reshape(head_shape)
    value_heads = qkv_vals[:, :, 2 * model_width :].reshape(head_shape)
    scores = attention_scores(query_heads, key_heads, valid_slots, score_scale)
    row_max = jnp.max(scores, axis=-1, keepdims=True)
    exponent = jnp.exp(scores - row_max)
    row_total = jnp.sum(exponent, axis=-1, keepdims=True)
    log_total = row_max + jnp.log(row_total)
    attention = (exponent / row_total).astype(jnp.bfloat16)
    attended = jnp.einsum(
        "fhqk,fkhs->fqhs", attention, value_heads, preferred_element_type=jnp.float32
    )
    attended = attended.reshape(frame_count, frame_len, model_width).astype(jnp.bfloat16)
    branch = (
        jnp.einsum("fbd,de->fbe", attended, out_low, preferred_element_type=jnp.float32) + out_bias
    )
    midway = frames_f + gate_attn * branch
    norm_two = modulate(midway, shift_mlp, scale_mlp).astype(jnp.bfloat16)
    up_values = (
        jnp.einsum("fbd,de->fbe", norm_two, up_low, preferred_element_type=jnp.float32) + up_bias
    )
    activated = gelu_tanh(up_values).astype(jnp.bfloat16)
    down_values = (
        jnp.einsum("fbe,ed->fbd", activated, down_low, preferred_element_type=jnp.float32)
        + down_bias
    )
    block_out = ((midway + gate_mlp * down_values) * row_mask).astype(jnp.bfloat16)
    regathered = (
        lax.all_gather(mod_weight.astype(jnp.bfloat16), ("wide", "narrow"), axis=0, tiled=True),
        lax.all_gather(qkv_weight.astype(jnp.bfloat16), ("wide", "narrow"), axis=0, tiled=True),
        lax.all_gather(out_weight.astype(jnp.bfloat16), ("wide", "narrow"), axis=0, tiled=True),
        lax.all_gather(up_weight.astype(jnp.bfloat16), ("wide", "narrow"), axis=0, tiled=True),
        lax.all_gather(down_weight.astype(jnp.bfloat16), ("wide", "narrow"), axis=0, tiled=True),
        lax.all_gather(biases.astype(jnp.bfloat16), ("wide", "narrow"), axis=0, tiled=True),
    )
    mod_low, qkv_low, out_low, up_low, down_low, bias_low = regathered
    upstream = cotangent.astype(jnp.float32) * row_mask
    d_gate_mlp = jnp.sum(upstream * down_values, axis=1, keepdims=True)
    d_down = (upstream * gate_mlp).astype(jnp.bfloat16)
    grad_down = jnp.einsum("fbe,fbd->ed", activated, d_down, preferred_element_type=jnp.float32)
    grad_down_bias = token_sum(d_down)
    d_activated = jnp.einsum("fbd,ed->fbe", d_down, down_low, preferred_element_type=jnp.float32)
    gelu_pull = jax.vjp(gelu_tanh, up_values)[1]
    d_up = gelu_pull(d_activated)[0].astype(jnp.bfloat16)
    grad_up = jnp.einsum("fbd,fbe->de", norm_two, d_up, preferred_element_type=jnp.float32)
    grad_up_bias = token_sum(d_up)
    d_norm_two = jnp.einsum("fbe,de->fbd", d_up, up_low, preferred_element_type=jnp.float32)
    second_pull = jax.vjp(modulate, midway, shift_mlp, scale_mlp)[1]
    d_midway, d_shift_mlp, d_scale_mlp = second_pull(d_norm_two)
    d_midway = d_midway + upstream
    d_gate_attn = jnp.sum(d_midway * branch, axis=1, keepdims=True)
    d_branch = (d_midway * gate_attn).astype(jnp.bfloat16)
    grad_out = jnp.einsum("fbd,fbe->de", attended, d_branch, preferred_element_type=jnp.float32)
    grad_out_bias = token_sum(d_branch)
    d_attended = jnp.einsum("fbe,de->fbd", d_branch, out_low, preferred_element_type=jnp.float32)
    d_attended = d_attended.astype(jnp.bfloat16).reshape(head_shape)
    scores = attention_scores(query_heads, key_heads, valid_slots, score_scale)
    soft = jnp.exp(scores - log_total)
    soft_low = soft.astype(jnp.bfloat16)
    d_soft = jnp.einsum(
        "fqhs,fkhs->fhqk", d_attended, value_heads, preferred_element_type=jnp.float32
    )
    d_value_heads = jnp.einsum(
        "fhqk,fqhs->fkhs", soft_low, d_attended, preferred_element_type=jnp.float32
    )
    d_scores = (soft * (d_soft - jnp.sum(soft * d_soft, axis=-1, keepdims=True))).astype(
        jnp.bfloat16
    )
    d_query_heads = (
        jnp.einsum("fhqk,fkhs->fqhs", d_scores, key_heads, preferred_element_type=jnp.float32)
        * score_scale
    )
    d_key_heads = (
        jnp.einsum("fhqk,fqhs->fkhs", d_scores, query_heads, preferred_element_type=jnp.float32)
        * score_scale
    )
    flat_shape = (frame_count, frame_len, model_width)
    d_qkv = jnp.concatenate(
        [
            d_query_heads.reshape(flat_shape),
            d_key_heads.reshape(flat_shape),
            d_value_heads.reshape(flat_shape),
        ],
        axis=-1,
    ).astype(jnp.bfloat16)
    grad_qkv = jnp.einsum("fbd,fbe->de", norm_one, d_qkv, preferred_element_type=jnp.float32)
    grad_query_bias = token_sum(d_qkv[:, :, :model_width])
    grad_value_bias = token_sum(d_qkv[:, :, 2 * model_width :])
    d_norm_one = jnp.einsum("fbe,de->fbd", d_qkv, qkv_low, preferred_element_type=jnp.float32)
    first_pull = jax.vjp(modulate, frames_f, shift_attn, scale_attn)[1]
    d_frames, d_shift_attn, d_scale_attn = first_pull(d_norm_one)
    frames_grad = (d_frames + d_midway).astype(jnp.bfloat16)
    d_modulation = jnp.concatenate(
        [d_shift_attn, d_scale_attn, d_gate_attn, d_shift_mlp, d_scale_mlp, d_gate_mlp], axis=-1
    )
    d_modulation = d_modulation[:, 0, :].astype(jnp.bfloat16)
    grad_mod = jnp.einsum("fd,fe->de", silu_low, d_modulation, preferred_element_type=jnp.float32)
    grad_mod_bias = jnp.sum(d_modulation, axis=0, dtype=jnp.float32)
    d_silu = jnp.einsum("fe,de->fd", d_modulation, mod_low, preferred_element_type=jnp.float32)
    silu_pull = jax.vjp(silu_act, cond_f)[1]
    cond_grad = silu_pull(d_silu)[0]
    grad_bias = jnp.concatenate(
        [
            grad_mod_bias,
            grad_query_bias,
            grad_value_bias,
            grad_out_bias,
            grad_up_bias,
            grad_down_bias,
        ]
    )
    all_sent = (
        lax.all_to_all(
            owner_split(grad_mod, owner_count).astype(jnp.bfloat16),
            ("wide", "narrow"),
            split_axis=0,
            concat_axis=0,
            tiled=True,
        ).astype(jnp.float32),
        lax.all_to_all(
            owner_split(grad_qkv, owner_count).astype(jnp.bfloat16),
            ("wide", "narrow"),
            split_axis=0,
            concat_axis=0,
            tiled=True,
        ).astype(jnp.float32),
        lax.all_to_all(
            owner_split(grad_out, owner_count).astype(jnp.bfloat16),
            ("wide", "narrow"),
            split_axis=0,
            concat_axis=0,
            tiled=True,
        ).astype(jnp.float32),
        lax.all_to_all(
            owner_split(grad_up, owner_count).astype(jnp.bfloat16),
            ("wide", "narrow"),
            split_axis=0,
            concat_axis=0,
            tiled=True,
        ).astype(jnp.float32),
        lax.all_to_all(
            owner_split(grad_down, owner_count).astype(jnp.bfloat16),
            ("wide", "narrow"),
            split_axis=0,
            concat_axis=0,
            tiled=True,
        ).astype(jnp.float32),
        lax.all_to_all(
            owner_split(grad_bias, owner_count).astype(jnp.bfloat16),
            ("wide", "narrow"),
            split_axis=0,
            concat_axis=0,
            tiled=True,
        ).astype(jnp.float32),
    )
    red_mod, red_qkv, red_out, red_up, red_down, red_bias = (
        source_sum(member, 0) for member in all_sent
    )
    reduced = (red_mod, red_qkv, red_out, red_up, red_down, red_bias)
    partial_sq = sum((jnp.sum(member * member) for member in reduced))
    total_sq = lax.psum(partial_sq, ("wide", "narrow"))
    grad_norm = jnp.sqrt(total_sq)
    factor = jnp.minimum(1.0, CLIP / (grad_norm + 1e-06))
    clipped = tuple((member * factor for member in reduced))
    masters = (mod_weight, qkv_weight, out_weight, up_weight, down_weight, biases)
    states = (mod_state, qkv_state, out_state, up_state, down_state, bias_state)
    updated = [adam_update(masters[index], states[index], clipped[index]) for index in range(6)]
    return (
        block_out,
        frames_grad,
        cond_grad,
        grad_norm,
        clipped[0],
        clipped[1],
        clipped[2],
        clipped[3],
        clipped[4],
        clipped[5],
        updated[0][0],
        updated[1][0],
        updated[2][0],
        updated[3][0],
        updated[4][0],
        updated[5][0],
        updated[0][1],
        updated[1][1],
        updated[2][1],
        updated[3][1],
        updated[4][1],
        updated[5][1],
    )


def solution(mesh):
    in_specs = (
        P(("wide", "narrow"), None, None),
        P(("wide", "narrow"), None),
        P(("wide", "narrow"), None),
        P(("wide", "narrow"), None, None),
        P(("wide", "narrow"), None),
        P(("wide", "narrow"), None),
        P(("wide", "narrow"), None),
        P(("wide", "narrow"), None),
        P(("wide", "narrow"), None),
        P(("wide", "narrow")),
        P(None, ("wide", "narrow"), None),
        P(None, ("wide", "narrow"), None),
        P(None, ("wide", "narrow"), None),
        P(None, ("wide", "narrow"), None),
        P(None, ("wide", "narrow"), None),
        P(None, ("wide", "narrow")),
    )
    out_specs = (
        P(("wide", "narrow"), None, None),
        P(("wide", "narrow"), None, None),
        P(("wide", "narrow"), None),
        P(),
        P(("wide", "narrow"), None),
        P(("wide", "narrow"), None),
        P(("wide", "narrow"), None),
        P(("wide", "narrow"), None),
        P(("wide", "narrow"), None),
        P(("wide", "narrow")),
        P(("wide", "narrow"), None),
        P(("wide", "narrow"), None),
        P(("wide", "narrow"), None),
        P(("wide", "narrow"), None),
        P(("wide", "narrow"), None),
        P(("wide", "narrow")),
        P(None, ("wide", "narrow"), None),
        P(None, ("wide", "narrow"), None),
        P(None, ("wide", "narrow"), None),
        P(None, ("wide", "narrow"), None),
        P(None, ("wide", "narrow"), None),
        P(None, ("wide", "narrow")),
    )
    return jax.shard_map(shards, mesh=mesh, in_specs=in_specs, out_specs=out_specs, check_vma=False)
```

profile of v0, /device:TPU:0, one launch (start us, length us, event | category | flops | bytes accessed | tf_op | source)
XLA Modules:
  0.0 1845.3 jit_solution(4483163921314430453)
XLA Ops:
  14.9 42.4 %all-reduce = bf16[16128]{0:T(1024)(128)(2,1)S(1)} all-reduce(bf16[16128]{0:T(1024)(128)(2,1)S(1)} %dynamic-update-slice), channel_id=1, replica_groups=mesh['wide'=16,'narrow'=2] {'wide','narrow'}, use_global_device_ids=true, to_apply=%add | all-reduce | flops 16128 | bytes 64512
  62.0 11.1 all-gather.16.cloned.1.call-done
  78.3 76.6 %all-gather.14.cloned.1.call-done = bf16[32,36,3456]{2,1,0:T(8,128)(2,1)} async-done(((bf16[1,36,3456]{2,1,0:T(8,128)(2,1)}), bf16[32,36,3456]{2,1,0:T(8,128)(2,1)}) %all-gather.14.cloned.1.call-update) | async-done | bytes 7962640 | tf_op jit(solution)/shard_map/all_gather | solution.py:116
  154.9 12.5 reshape.734
  167.5 82.0 %all-gather.18.cloned.1.call-done = bf16[32,36,4608]{2,1,0:T(8,128)(2,1)} async-done(((bf16[1,36,4608]{2,1,0:T(8,128)(2,1)}), bf16[32,36,4608]{2,1,0:T(8,128)(2,1)}) %all-gather.18.cloned.1.call-update) | async-done | bytes 10616848 | tf_op jit(solution)/shard_map/all_gather | solution.py:118
  249.5 14.0 reshape.738
  263.5 106.9 %all-gather.12.cloned.1.call-done = bf16[32,36,6912]{2,1,0:T(8,128)(2,1)} async-done(((bf16[1,36,6912]{2,1,0:T(8,128)(2,1)}), bf16[32,36,6912]{2,1,0:T(8,128)(2,1)}) %all-gather.12.cloned.1.call-update) | async-done | bytes 15925264 | tf_op jit(solution)/shard_map/all_gather | solution.py:115
  370.5 18.5 reshape.732
  388.9 7.9 convolution_reduce_fusion
  410.7 6.5 fusion.13
  417.3 42.1 %all-gather.10.cloned.1.call-done = bf16[4608,1152]{1,0:T(8,128)(2,1)} async-done(((bf16[144,1152]{1,0:T(8,128)(2,1)}), bf16[4608,1152]{1,0:T(8,128)(2,1)}) %all-gather.10.cloned.1.call-update) | async-done | bytes 10616848 | tf_op jit(solution)/shard_map/all_gather | solution.py:119
  459.4 10.0 fusion.161
  469.3 7.6 fusion.160
  499.0 6.3 fusion.44
  513.8 11.6 fusion.45
  558.4 7.4 convolution_convert_fusion.2
  565.8 55.5 %all-to-all-done.2 = bf16[32,36,1152]{2,1,0:T(8,128)(2,1)S(1)} async-done(((bf16[32,36,1152]{2,1,0:T(8,128)(2,1)}), bf16[32,36,1152]{2,1,0:T(8,128)(2,1)S(1)}, u32[]{:S(2)}, u32[]{:S(2)}) %all-to-all-start.2) | async-done | bytes 2654240 | tf_op jit(solution)/shard_map/all_to_all | solution.py:266
  627.5 9.5 convolution_convert_fusion.1
  637.0 182.2 %all-to-all-done.1 = bf16[32,36,3456]{2,1,0:T(8,128)(2,1)} async-done(((bf16[32,36,3456]{2,1,0:T(8,128)(2,1)}), bf16[32,36,3456]{2,1,0:T(8,128)(2,1)}, u32[]{:S(2)}, u32[]{:S(2)}) %all-to-all-start.1) | async-done | bytes 7962656 | tf_op jit(solution)/shard_map/all_to_all | solution.py:259
  819.2 7.8 all-to-all-start.3
  831.4 9.1 convolution_convert_fusion
  840.5 244.4 %all-to-all-done.3 = bf16[32,36,4608]{2,1,0:T(8,128)(2,1)} async-done(((bf16[32,36,4608]{2,1,0:T(8,128)(2,1)}), bf16[32,36,4608]{2,1,0:T(8,128)(2,1)}, u32[]{:S(2)}, u32[]{:S(2)}) %all-to-all-start.3) | async-done | bytes 10616864 | tf_op jit(solution)/shard_map/all_to_all | solution.py:273
  1084.9 12.0 all-to-all-start.4
  1098.7 6.4 multiply_convert_fusion
  1105.1 224.1 %all-to-all-done.4 = bf16[32,144,1152]{2,1,0:T(8,128)(2,1)} async-done(((bf16[32,144,1152]{2,1,0:T(8,128)(2,1)}), bf16[32,144,1152]{2,1,0:T(8,128)(2,1)}, u32[]{:S(2)}, u32[]{:S(2)}) %all-to-all-start.4) | async-done | bytes 10616864 | tf_op jit(solution)/shard_map/all_to_all | solution.py:280
  1329.2 10.4 all-to-all-start
  1347.3 6.0 convert_reduce_fusion.2
  1354.1 6.5 convert_reduce_fusion.1
  1361.3 363.7 %all-to-all-done = bf16[32,36,6912]{2,1,0:T(8,128)(2,1)} async-done(((bf16[32,36,6912]{2,1,0:T(8,128)(2,1)}), bf16[32,36,6912]{2,1,0:T(8,128)(2,1)}, u32[]{:S(2)}, u32[]{:S(2)}) %all-to-all-start) | async-done | bytes 15925280 | tf_op jit(solution)/shard_map/all_to_all | solution.py:252
  1725.1 19.6 %convert_reduce_fusion = f32[36,6912]{1,0:T(8,128)S(1)} fusion(bf16[32,36,6912]{2,1,0:T(8,128)(2,1)} %all-to-all-done), kind=kLoop, calls=%fused_computation.1 | loop fusion | flops 15676416 | bytes 16920576 | tf_op jit(solution)/shard_map/reduce_sum | solution.py:87
  1749.4 10.4 fusion.119
  1759.8 52.7 %psum.7 = f32[]{:T(128)} all-reduce(f32[]{:T(128)S(6)} %add.341), channel_id=1, replica_groups=mesh['wide'=16,'narrow'=2] {'wide','narrow'}, use_global_device_ids=true, to_apply=%region_34.35 | all-reduce | flops 1 | bytes 8 | tf_op jit(solution)/shard_map/psum | solution.py:300
  (300 shorter events, 139.5 us)
Async XLA Ops:
  7.2 66.0 %all-gather.16.cloned.1.call-start = ((), (), s32[]{:S(2)}) async-start(), calls=%async_computation.9 | async-start | bytes 3041280 | tf_op jit(solution)/shard_map/all_gather | solution.py:117
  8.9 146.0 %all-gather.14.cloned.1.call-start = ((), (), s32[]{:S(2)}) async-start(), calls=%async_computation.8 | async-start | bytes 9123840 | tf_op jit(solution)/shard_map/all_gather | solution.py:116
  10.8 238.7 %all-gather.18.cloned.1.call-start = ((), (), s32[]{:S(2)}) async-start(), calls=%async_computation.10 | async-start | bytes 12165120 | tf_op jit(solution)/shard_map/all_gather | solution.py:118
  12.8 45.1 %copy-start.75 = (s32[1,2]{1,0:T(1,128)S(1)}, s32[1,2]{1,0:T(1,128)}, u32[]{:S(2)}) copy-start(s32[1,2]{1,0:T(1,128)} %param.18) | copy-start | bytes 28
  12.8 48.7 %copy-start.5 = (bf16[1,256,1152]{2,1,0:T(8,128)(2,1)S(1)}, bf16[1,256,1152]{2,1,0:T(8,128)(2,1)}, u32[]{:S(2)}) copy-start(bf16[1,256,1152]{2,1,0:T(8,128)(2,1)} %param.16) | copy-start | bytes 1769476
  12.8 357.6 %all-gather.12.cloned.1.call-start = ((), (), s32[]{:S(2)}) async-start(), calls=%async_computation.7 | async-start | bytes 18247680 | tf_op jit(solution)/shard_map/all_gather | solution.py:115
  13.8 445.6 %all-gather.10.cloned.1.call-start = ((), (), s32[]{:S(2)}) async-start(), calls=%async_computation.6 | async-start | bytes 10948608 | tf_op jit(solution)/shard_map/all_gather | solution.py:119
  61.7 335.8 %copy-start.60 = (f32[256]{0:T(256)}, f32[256]{0:T(256)S(1)}, u32[]{:S(2)}) copy-start(f32[256]{0:T(256)S(1)} %broadcast_multiply_fusion.7) | copy-start | bytes 3076
  62.0 16.3 copy-start.63
  62.0 335.5 %copy-start.62 = (f32[256]{0:T(256)}, f32[256]{0:T(256)S(1)}, u32[]{:S(2)}) copy-start(f32[256]{0:T(256)S(1)} %fusion.134) | copy-start | bytes 3076
  263.5 125.4 %copy-start.41 = (bf16[1,1152]{1,0:T(2,128)(2,1)S(1)}, bf16[1,1152]{1,0:T(2,128)(2,1)}, u32[]{:S(2)}) copy-start(bf16[1,1152]{1,0:T(2,128)(2,1)} %param.17) | copy-start | bytes 6916
  388.9 8.6 copy-start.7
  397.5 8.5 copy-start.39
  403.0 7.7 slice-start
  410.7 48.6 %copy-start.25 = (bf16[1,256,1152]{2,1,0:T(8,128)(2,1)S(1)}, bf16[1,256,1152]{2,1,0:T(8,128)(2,1)}, u32[]{:S(2)}) copy-start(bf16[1,256,1152]{2,1,0:T(8,128)(2,1)} %param.19) | copy-start | bytes 1769476
  469.3 7.6 copy-start.68
  505.9 7.9 copy-start.38
  513.8 12.2 copy-start.51
  513.8 12.8 copy-start.43
  540.5 10.4 all-to-all-start.5
  551.5 69.9 %all-to-all-start.2 = ((bf16[32,36,1152]{2,1,0:T(8,128)(2,1)}), bf16[32,36,1152]{2,1,0:T(8,128)(2,1)S(1)}, u32[]{:S(2)}, u32[]{:S(2)}) async-start(bf16[32,36,1152]{2,1,0:T(8,128)(2,1)} %convolution_convert_fusion.3), calls=%async_computation.2 | async-start | bytes 5898240 | tf_op jit(solution)/shard_map/all_to_all | solution.py:266
  621.3 197.9 %all-to-all-start.1 = ((bf16[32,36,3456]{2,1,0:T(8,128)(2,1)}), bf16[32,36,3456]{2,1,0:T(8,128)(2,1)}, u32[]{:S(2)}, u32[]{:S(2)}) async-start(bf16[32,36,3456]{2,1,0:T(8,128)(2,1)} %convolution_convert_fusion.2), calls=%async_computation.1 | async-start | bytes 17694720 | tf_op jit(solution)/shard_map/all_to_all | solution.py:259
  819.2 265.6 %all-to-all-start.3 = ((bf16[32,36,4608]{2,1,0:T(8,128)(2,1)}), bf16[32,36,4608]{2,1,0:T(8,128)(2,1)}, u32[]{:S(2)}, u32[]{:S(2)}) async-start(bf16[32,36,4608]{2,1,0:T(8,128)(2,1)} %convolution_convert_fusion.1), calls=%async_computation.3 | async-start | bytes 23592960 | tf_op jit(solution)/shard_map/all_to_all | solution.py:273
  840.5 256.4 %copy-start.42 = (bf16[1,1152]{1,0:T(2,128)(2,1)S(1)}, bf16[1,1152]{1,0:T(2,128)(2,1)}, u32[]{:S(2)}) copy-start(bf16[1,1152]{1,0:T(2,128)(2,1)} %param.17) | copy-start | bytes 6916
  840.5 256.9 %copy-start.45 = (bf16[1152]{0:T(1024)(128)(2,1)S(1)}, bf16[1152]{0:T(1024)(128)(2,1)}, u32[]{:S(2)}) copy-start(bf16[1152]{0:T(1024)(128)(2,1)} %copy-done.44) | copy-start | bytes 6916
  840.5 257.1 %copy-start.56 = (bf16[1152]{0:T(1024)(128)(2,1)S(1)}, bf16[1152]{0:T(1024)(128)(2,1)}, u32[]{:S(2)}) copy-start(bf16[1152]{0:T(1024)(128)(2,1)} %copy-done.55) | copy-start | bytes 6916
  840.5 257.4 %copy-start.52 = (bf16[1152]{0:T(1024)(128)(2,1)S(1)}, bf16[1152]{0:T(1024)(128)(2,1)}, u32[]{:S(2)}) copy-start(bf16[1152]{0:T(1024)(128)(2,1)} %get-tuple-element.89) | copy-start | bytes 6916
  840.5 258.0 %copy-start.54 = (bf16[1152]{0:T(1024)(128)(2,1)S(1)}, bf16[1152]{0:T(1024)(128)(2,1)}, u32[]{:S(2)}) copy-start(bf16[1152]{0:T(1024)(128)(2,1)} %copy-done.53) | copy-start | bytes 6916
  1084.9 244.3 %all-to-all-start.4 = ((bf16[32,144,1152]{2,1,0:T(8,128)(2,1)}), bf16[32,144,1152]{2,1,0:T(8,128)(2,1)}, u32[]{:S(2)}, u32[]{:S(2)}) async-start(bf16[32,144,1152]{2,1,0:T(8,128)(2,1)} %convolution_convert_fusion), calls=%async_computation.4 | async-start | bytes 21233664 | tf_op jit(solution)/shard_map/all_to_all | solution.py:280
  1105.1 234.5 %copy-start.59 = (f32[3,504]{1,0:T(4,128)S(1)}, f32[3,504]{1,0:T(4,128)}, u32[]{:S(2)}) copy-start(f32[3,504]{1,0:T(4,128)} %param.31) | copy-start | bytes 18148
  1105.1 234.5 %copy-start.36 = (bf16[32,2,252]{2,1,0:T(2,128)(2,1)S(1)}, bf16[32,2,252]{2,1,0:T(2,128)(2,1)}, u32[]{:S(2)}) copy-start(bf16[32,2,252]{2,1,0:T(2,128)(2,1)} %copy-done.35) | copy-start | bytes 96772
  1329.2 395.9 %all-to-all-start = ((bf16[32,36,6912]{2,1,0:T(8,128)(2,1)}), bf16[32,36,6912]{2,1,0:T(8,128)(2,1)}, u32[]{:S(2)}, u32[]{:S(2)}) async-start(bf16[32,36,6912]{2,1,0:T(8,128)(2,1)} %multiply_convert_fusion), calls=%async_computation | async-start | bytes 35389440 | tf_op jit(solution)/shard_map/all_to_all | solution.py:252
  (58 other events, 165.1 us)
Sparse Core Ops, SparseCore 0:
  11.5 61.6 all-gather.15
  76.7 78.2 all-gather.13
  158.4 90.9 all-gather.17
  252.8 117.5 all-gather.11
  373.8 85.5 all-gather.9
where the time goes:
time: 1860 us; the launch traced here: 1850 us
  waiting for transfers between devices  1390 us (75%)
  matrix products  109 us (6%)
  local copies, waits for them, and re-layouts  102 us (5%)
  blocking collectives  95.1 us (5%)
  other arithmetic  84.9 us (5%)
  starting transfers between devices  40.1 us (2%)
  between operations  22.2 us (1%)
    all_to_all x1, waiting for transfers between devices, shards(): lax.all_to_all(owner_split(grad_mod, owner_count).astype(jnp.bfloat16), (...  364 us
    all_to_all x1, waiting for transfers between devices, shards(): lax.all_to_all(owner_split(grad_up, owner_count).astype(jnp.bfloat16), ('...  244 us
    all_to_all x1, waiting for transfers between devices, shards(): lax.all_to_all(owner_split(grad_down, owner_count).astype(jnp.bfloat16),...  224 us
    all_to_all x1, waiting for transfers between devices, shards(): lax.all_to_all(owner_split(grad_qkv, owner_count).astype(jnp.bfloat16), (...  182 us
    all_gather x1, waiting for transfers between devices, shards(): lax.all_gather(mod_weight.astype(jnp.bfloat16), ('wide', 'narrow'), axis=...  107 us
    all_gather x1, waiting for transfers between devices, shards(): lax.all_gather(up_weight.astype(jnp.bfloat16), ('wide', 'narrow'), axis=0...  82 us
    all_gather x1, waiting for transfers between devices, shards(): lax.all_gather(qkv_weight.astype(jnp.bfloat16), ('wide', 'narrow'), axis=...  76.6 us
    unnamed x181, local copies, waits for them, and re-layouts  75.7 us
  transfers between devices with their start and end apart: 11, of which 11 were waited for; matrix products, arithmetic and copies ran while one was open for 8% of the time, Pallas kernels for 0%

commit v1 on v0

v1 whole, which is shorter than its diff:
```python
import functools
import jax
import jax.numpy as jnp
from jax import lax
from jax.experimental import pallas as pl
from jax.experimental.pallas import tpu as pltpu
from jax.sharding import PartitionSpec as P

HEADS = 16
STEPS = 4
CLIP = 576
NORM_EPS = 1e-06
RATE = 0.04
FIRST_DECAY = 0.5
SECOND_DECAY = 0.5
WEIGHT_DECAY = 0.1
ADAM_EPS = 1e-08
AVERAGE_DECAY = 0.9999
MASK_VALUE = -1e30
AXES = ("wide", "narrow")

MESH = pl.DeviceIdType.MESH
CORE = 1


def orders(bits, late):
    high = list(range(bits - 1, 2, -1))
    if late:
        pair = (high[:-1] + [0, 2] + high[-1:], high[:-1] + [2, 0] + high[-1:])
    else:
        pair = (high + [2, 0], high + [0, 2])
    return tuple(order + [CORE] for order in pair)


def masks(order, member):
    return sum(1 << bit for place, bit in enumerate(order) if member >> place & 1)


def me_index():
    return lax.axis_index("wide") * 2 + lax.axis_index("narrow")


def device(index):
    return (index // 2, lax.rem(index, 2))


def own_plane(me):
    return lax.rem(me // 2, 2)


def flip(index, mask):
    out = index
    bit = 0
    while mask >> bit:
        if mask >> bit & 1:
            value = lax.rem(out // (1 << bit), 2)
            out = out + (1 << bit) * (1 - 2 * value)
        bit += 1
    return out


def block_of(me, pair, member, bits):
    plane = own_plane(me)
    last = 1 << (bits - 1)
    if member & last:
        rest = member - last
        zero = flip(flip(me, 1 << CORE), masks(pair[1], rest))
        one = flip(flip(me, 1 << CORE), masks(pair[0], rest))
    else:
        zero = flip(me, masks(pair[0], member))
        one = flip(me, masks(pair[1], member))
    return jnp.where(plane == 0, zero, one)


def partner_of(me, pair, place):
    zero = flip(me, 1 << pair[0][place])
    if pair[0][place] == pair[1][place]:
        return zero
    return jnp.where(own_plane(me) == 0, zero, flip(me, 1 << pair[1][place]))


def greet(me, bits):
    barrier = pltpu.get_barrier_semaphore()
    partners = [flip(me, 1 << bit) for bit in range(bits)] + [flip(me, 3)]
    for partner in partners:
        pl.semaphore_signal(barrier, inc=1, device_id=device(partner), device_id_type=MESH)
    pl.semaphore_wait(barrier, len(partners))


def top_place(member):
    return member.bit_length() - 1


def gather_kernel(bits, rows, lates, a_src, b_src, c_src, a_out, b_out, c_out,
                  stage, block, c_block, quad_send, quad_recv, own_sem, keep_sem, send_sem, recv_sem):
    count = 1 << bits
    me = me_index()
    quad, spot = lax.rem(me, 4), me // 4
    pairs = [orders(bits, late) for late in lates]
    outs = (a_out, b_out, c_out)

    def place(kind, index):
        q, j = lax.rem(index, 4), index // 4
        return outs[kind].at[q, j] if kind < 2 else outs[kind].at[j, q]

    def send(kind, member, step, source):
        target = member | 1 << step
        return pltpu.make_async_remote_copy(
            src_ref=source,
            dst_ref=place(kind, block_of(me, pairs[kind], member, bits)),
            send_sem=send_sem.at[kind, target],
            recv_sem=recv_sem.at[kind, target],
            device_id=device(partner_of(me, pairs[kind], step)),
            device_id_type=MESH,
        )

    own = []
    for kind, source in enumerate((a_src, b_src)):
        own.append(pltpu.make_async_copy(source.at[quad], stage.at[kind, quad], own_sem.at[kind]))
    own.append(pltpu.make_async_copy(c_src, c_block, own_sem.at[2]))
    for copy in own:
        copy.start()
    greet(me, bits)
    quads = []
    for kind, source in enumerate((a_src, b_src)):
        for other in (1, 2, 3):
            copy = pltpu.make_async_remote_copy(
                src_ref=source.at[flip(quad, other)],
                dst_ref=stage.at[kind, quad],
                send_sem=quad_send.at[kind, other],
                recv_sem=quad_recv.at[kind, other],
                device_id=device(flip(me, other)),
                device_id_type=MESH,
            )
            copy.start()
            quads.append(copy)
    sends = []
    keeps = []

    def launch(kind, member, source):
        for step in range(top_place(member) + 1, bits):
            copy = send(kind, member, step, source)
            copy.start()
            sends.append(copy)

    def keep(kind, source):
        copy = pltpu.make_async_copy(source, place(kind, me), keep_sem.at[kind])
        copy.start()
        keeps.append(copy)

    own[2].wait()
    launch(2, 0, c_block)
    keep(2, c_block)
    padded = block.shape[1]
    for kind in (0, 1):
        own[kind].wait()
        for copy in quads[3 * kind:3 * kind + 3]:
            copy.wait_recv()
        for lane in range(0, stage.shape[3], 128):
            parts = [stage[kind, q, :, lane:lane + 128].astype(jnp.float32) for q in range(4)]
            if padded > 4 * rows:
                parts.append(jnp.zeros((padded - 4 * rows, 128), jnp.float32))
            block[kind, :, lane:lane + 128] = jnp.concatenate(parts, axis=0).astype(jnp.bfloat16)
        launch(kind, 0, block.at[kind])
        keep(kind, block.at[kind])

    def arrived(kind, member):
        spot_ref = place(kind, block_of(me, pairs[kind], member, bits))
        pltpu.make_async_copy(spot_ref, spot_ref, recv_sem.at[kind, member]).wait()
        return spot_ref

    for member in range(1, count):
        for kind in (2, 0, 1):
            launch(kind, member, arrived(kind, member))
    for copy in sends + quads:
        copy.wait_send()
    for copy in keeps:
        copy.wait()


def gather(a_src, b_src, c_src, count, lates=(False, False, False)):
    bits = count.bit_length() - 1
    rows, columns = a_src.shape[1:]
    padded = -(-4 * rows // 16) * 16
    c_padded = -(-c_src.shape[0] // 16) * 16
    if c_padded != c_src.shape[0]:
        c_src = jnp.pad(c_src, ((0, c_padded - c_src.shape[0]), (0, 0)))
    kinds = 3
    anywhere = pl.BlockSpec(memory_space=pl.ANY)
    big = jax.ShapeDtypeStruct((4, count // 4, padded, columns), jnp.bfloat16)
    tall = jax.ShapeDtypeStruct((count // 4, 4, c_padded, columns), jnp.bfloat16)
    a_all, b_all, c_all = pl.pallas_call(
        functools.partial(gather_kernel, bits, rows, lates),
        out_shape=(big, big, tall),
        in_specs=[anywhere] * 3,
        out_specs=(anywhere,) * 3,
        scratch_shapes=[
            pltpu.VMEM((2, 4, rows, columns), jnp.bfloat16),
            pltpu.VMEM((2, padded, columns), jnp.bfloat16),
            pltpu.VMEM((c_padded, columns), jnp.bfloat16),
            pltpu.SemaphoreType.DMA((2, 4)),
            pltpu.SemaphoreType.DMA((2, 4)),
            pltpu.SemaphoreType.DMA((3,)),
            pltpu.SemaphoreType.DMA((3,)),
            pltpu.SemaphoreType.DMA((kinds, count)),
            pltpu.SemaphoreType.DMA((kinds, count)),
        ],
        compiler_params=pltpu.CompilerParams(collective_id=0, has_side_effects=True),
        cost_estimate=pl.CostEstimate(flops=0, bytes_accessed=400_000_000, transcendentals=0),
        name="gather_weights",
    )(a_src, b_src, c_src)
    return a_all, b_all, c_all


def reduce_kernel(bits, rows, lates, a_in, b_in, c_in, a_out, b_out, c_out,
                  own, recv, quad_block, total, own_sem, send_sem, recv_sem, quad_send, quad_recv, quad_own, total_sem):
    count = 1 << bits
    half = count // 2
    me = me_index()
    quad = lax.rem(me, 4)
    pairs = [orders(bits, late) for late in lates]
    ins = (a_in, b_in, c_in)
    kinds = (2, 1, 0)

    def place(kind, index):
        q, j = lax.rem(index, 4), index // 4
        return ins[kind].at[q, j] if kind < 2 else ins[kind].at[j, q]

    loads = {}
    for member in range(half - 1, -1, -1):
        for kind in kinds:
            loads[kind, member] = pltpu.make_async_copy(
                place(kind, block_of(me, pairs[kind], member, bits)), own.at[kind, member], own_sem.at[kind, member]
            )
    sends = []

    def send(kind, member, source):
        step = top_place(member)
        copy = pltpu.make_async_remote_copy(
            src_ref=source,
            dst_ref=recv.at[kind, member],
            send_sem=send_sem.at[kind, member],
            recv_sem=recv_sem.at[kind, member],
            device_id=device(partner_of(me, pairs[kind], step)),
            device_id_type=MESH,
        )
        copy.start()
        sends.append(copy)

    for kind in kinds:
        loads[kind, half - 1].start()
    greet(me, bits)
    for member in range(half - 1, -1, -1):
        for kind in kinds:
            send(kind, member + half, place(kind, block_of(me, pairs[kind], member + half, bits)))
            if member < half - 1:
                loads[kind, member].start()

    padded, columns = own.shape[2:]

    def ready(kind, member):
        loads[kind, member].wait()
        parts = [member | 1 << step for step in range(top_place(member) + 1, bits)]
        for part in parts:
            pltpu.make_async_copy(recv.at[kind, part], recv.at[kind, part], recv_sem.at[kind, part]).wait()
        return parts

    def summed(kind, member, parts, where):
        value = own[kind, member, where, :].astype(jnp.float32)
        for part in parts:
            value = value + recv[kind, part, where, :].astype(jnp.float32)
        return value

    for member in range(half - 1, 0, -1):
        for kind in kinds:
            parts = ready(kind, member)

            def strip(s, carry, kind=kind, member=member, parts=parts):
                where = pl.ds(pl.multiple_of(s * 16, 16), 16)
                own[kind, member, where, :] = summed(kind, member, parts, where).astype(jnp.bfloat16)
                return carry

            lax.fori_loop(0, padded // 16, strip, 0)
            send(kind, member, own.at[kind, member])

    copies = []
    for kind in kinds:
        parts = ready(kind, 0)

        def strip(s, carry, kind=kind, parts=parts):
            where = pl.ds(pl.multiple_of(s * 16, 16), 16)
            total[kind, where, :] = summed(kind, 0, parts, where)
            return carry

        lax.fori_loop(0, padded // 16, strip, 0)
        if kind == 2:
            copy = pltpu.make_async_copy(total.at[2], c_out, total_sem)
            copy.start()
            copies.append(copy)
            continue
        out = (a_out, b_out)[kind]
        for lane in range(0, columns, 128):
            for q in range(4):
                quad_block[kind, q, :, lane:lane + 128] = total[kind, q * rows:(q + 1) * rows, lane:lane + 128].astype(jnp.bfloat16)
        copy = pltpu.make_async_copy(quad_block.at[kind, quad], out.at[quad], quad_own.at[kind])
        copy.start()
        copies.append(copy)
        for other in (1, 2, 3):
            copy = pltpu.make_async_remote_copy(
                src_ref=quad_block.at[kind, flip(quad, other)],
                dst_ref=out.at[quad],
                send_sem=quad_send.at[kind, other],
                recv_sem=quad_recv.at[kind, other],
                device_id=device(flip(me, other)),
                device_id_type=MESH,
            )
            copy.start()
            copies.append(copy)
    for copy in copies:
        copy.wait()
    for copy in sends:
        copy.wait_send()


def reduce(a_in, b_in, c_in, rows, lates=(False, False, False)):
    count = a_in.shape[1] * 4
    bits = count.bit_length() - 1
    padded, columns = a_in.shape[2:]
    anywhere = pl.BlockSpec(memory_space=pl.ANY)
    share = jax.ShapeDtypeStruct((4, rows, columns), jnp.bfloat16)
    return pl.pallas_call(
        functools.partial(reduce_kernel, bits, rows, lates),
        out_shape=(share, share, jax.ShapeDtypeStruct((padded, columns), jnp.float32)),
        in_specs=[anywhere] * 3,
        out_specs=(anywhere,) * 3,
        scratch_shapes=[
            pltpu.VMEM((3, count // 2, padded, columns), jnp.bfloat16),
            pltpu.VMEM((3, count, padded, columns), jnp.bfloat16),
            pltpu.VMEM((2, 4, rows, columns), jnp.bfloat16),
            pltpu.VMEM((3, padded, columns), jnp.float32),
            pltpu.SemaphoreType.DMA((3, count // 2)),
            pltpu.SemaphoreType.DMA((3, count)),
            pltpu.SemaphoreType.DMA((3, count)),
            pltpu.SemaphoreType.DMA((2, 4)),
            pltpu.SemaphoreType.DMA((2, 4)),
            pltpu.SemaphoreType.DMA((2,)),
            pltpu.SemaphoreType.DMA,
        ],
        compiler_params=pltpu.CompilerParams(collective_id=1, has_side_effects=True, vmem_limit_bytes=62 * 1024 * 1024),
        cost_estimate=pl.CostEstimate(flops=0, bytes_accessed=400_000_000, transcendentals=0),
        name="reduce_gradients",
    )(a_in, b_in, c_in)


def layer_norm(values):
    centre = jnp.mean(values, axis=-1, keepdims=True)
    centred = values - centre
    spread = jnp.mean(centred * centred, axis=-1, keepdims=True)
    return centred * lax.rsqrt(spread + NORM_EPS)


def modulate(values, shift_part, scale_part):
    return layer_norm(values) * (1.0 + scale_part) + shift_part


def silu_act(values):
    return values * jax.nn.sigmoid(values)


def gelu_tanh(values):
    inner = 0.7978845608028654 * (values + 0.044715 * values * values * values)
    return 0.5 * values * (1.0 + jnp.tanh(inner))


def slot_mask(grid, frame_len):
    area = grid[:, 0] * grid[:, 1]
    return lax.broadcasted_iota(jnp.int32, (grid.shape[0], frame_len), 1) < area[:, None]


def split_biases(biases, model_width, hidden_width):
    edges = [
        6 * model_width,
        7 * model_width,
        8 * model_width,
        9 * model_width,
        9 * model_width + hidden_width,
    ]
    return jnp.split(biases, edges)


def adam_update(weight, state, grad):
    first = FIRST_DECAY * state[0] + (1.0 - FIRST_DECAY) * grad
    second = SECOND_DECAY * state[1] + (1.0 - SECOND_DECAY) * grad * grad
    first_hat = first / (1.0 - FIRST_DECAY**STEPS)
    second_hat = second / (1.0 - SECOND_DECAY**STEPS)
    new_weight = weight - RATE * (
        first_hat / (jnp.sqrt(second_hat) + ADAM_EPS) + WEIGHT_DECAY * weight
    )
    average = AVERAGE_DECAY * state[2] + (1.0 - AVERAGE_DECAY) * new_weight
    return (new_weight, jnp.stack([first, second, average]))


def attention_scores(query_heads, key_heads, valid_slots, score_scale):
    scores = (
        jnp.einsum("fqhs,fkhs->fhqk", query_heads, key_heads, preferred_element_type=jnp.float32)
        * score_scale
    )
    return jnp.where(valid_slots[:, None, None, :], scores, MASK_VALUE)


def token_sum(values):
    return jnp.sum(values, axis=(0, 1), dtype=jnp.float32)


def exchange(packets):
    return lax.all_to_all(packets, AXES, split_axis=0, concat_axis=0, tiled=True)


def shards(
    frames_in,
    conditioning,
    grid,
    cotangent,
    mod_weight,
    qkv_weight,
    out_weight,
    up_weight,
    down_weight,
    biases,
    mod_state,
    qkv_state,
    out_state,
    up_state,
    down_state,
    bias_state,
):
    frame_count, frame_len, model_width = frames_in.shape
    hidden_width = up_weight.shape[1]
    head_size = model_width // HEADS
    score_scale = head_size ** (-0.5)
    head_shape = (frame_count, frame_len, HEADS, head_size)
    count = lax.axis_size("wide") * lax.axis_size("narrow")
    rows = mod_weight.shape[0]
    tall_rows = down_weight.shape[0]
    low = jnp.bfloat16

    def slices(member):
        return member.reshape(rows, 4, model_width).transpose(1, 0, 2)

    a_src = slices(jnp.concatenate([qkv_weight.astype(low), out_weight.astype(low)], axis=1))
    b_src = slices(up_weight.astype(low))
    a_all, b_all, c_all = gather(a_src, b_src, down_weight.astype(low), count, (False, False, True))
    a_all = a_all[:, :, : 4 * rows].reshape(4, model_width, model_width)
    up_low = b_all[:, :, : 4 * rows].reshape(4, model_width, model_width)
    down_low = c_all[:, :, :tall_rows].reshape(hidden_width, model_width)
    query_low, key_low, value_low, out_low = (a_all[index] for index in range(4))

    cond_f = conditioning.astype(jnp.float32)
    silu_low = silu_act(cond_f).astype(low)
    mod_low = mod_weight.astype(low)
    first = exchange(
        jnp.concatenate(
            [
                silu_low.reshape(count, rows),
                jnp.broadcast_to(biases.astype(low)[None], (count, biases.shape[0])),
            ],
            axis=1,
        )
    )
    silu_rows = first[:, :rows]
    bias_low = first[:, rows:].reshape(-1)
    mod_terms = exchange(jnp.dot(silu_rows, mod_low, preferred_element_type=jnp.float32))
    mod_bias, query_bias, value_bias, out_bias, up_bias, down_bias = split_biases(
        bias_low.astype(jnp.float32), model_width, hidden_width
    )
    modulation = jnp.sum(mod_terms, axis=0, keepdims=True) + mod_bias
    valid_slots = slot_mask(grid, frame_len)
    row_mask = valid_slots[:, :, None].astype(jnp.float32)
    frames_f = frames_in.astype(jnp.float32)
    shift_attn, scale_attn, gate_attn, shift_mlp, scale_mlp, gate_mlp = jnp.split(
        modulation[:, None, :], 6, axis=-1
    )
    norm_one = modulate(frames_f, shift_attn, scale_attn).astype(low)

    def project(values, weight):
        return jnp.einsum("fbd,de->fbe", values, weight, preferred_element_type=jnp.float32)

    query_heads = (project(norm_one, query_low) + query_bias).astype(low).reshape(head_shape)
    key_heads = project(norm_one, key_low).astype(low).reshape(head_shape)
    value_heads = (project(norm_one, value_low) + value_bias).astype(low).reshape(head_shape)
    scores = attention_scores(query_heads, key_heads, valid_slots, score_scale)
    row_max = jnp.max(scores, axis=-1, keepdims=True)
    exponent = jnp.exp(scores - row_max)
    row_total = jnp.sum(exponent, axis=-1, keepdims=True)
    log_total = row_max + jnp.log(row_total)
    attention = (exponent / row_total).astype(low)
    attended = jnp.einsum(
        "fhqk,fkhs->fqhs", attention, value_heads, preferred_element_type=jnp.float32
    )
    attended = attended.reshape(frame_count, frame_len, model_width).astype(low)
    branch = project(attended, out_low) + out_bias
    midway = frames_f + gate_attn * branch
    norm_two = modulate(midway, shift_mlp, scale_mlp).astype(low)
    up_values = (
        jnp.einsum("fbd,sde->fbse", norm_two, up_low, preferred_element_type=jnp.float32).reshape(
            frame_count, frame_len, hidden_width
        )
        + up_bias
    )
    activated = gelu_tanh(up_values).astype(low)
    down_values = project(activated, down_low) + down_bias
    block_out = ((midway + gate_mlp * down_values) * row_mask).astype(low)
    upstream = cotangent.astype(jnp.float32) * row_mask
    d_gate_mlp = jnp.sum(upstream * down_values, axis=1, keepdims=True)
    d_down = (upstream * gate_mlp).astype(low)
    grad_down = jnp.einsum("fbe,fbd->ed", activated, d_down, preferred_element_type=jnp.float32)
    grad_down_bias = token_sum(d_down)
    d_activated = jnp.einsum("fbd,ed->fbe", d_down, down_low, preferred_element_type=jnp.float32)
    gelu_pull = jax.vjp(gelu_tanh, up_values)[1]
    d_up = gelu_pull(d_activated)[0].astype(low)
    d_up_parts = d_up.reshape(frame_count, frame_len, 4, model_width)
    grad_up = jnp.einsum("fbd,fbse->sde", norm_two, d_up_parts, preferred_element_type=jnp.float32)
    grad_up_bias = token_sum(d_up)
    d_norm_two = jnp.einsum("fbse,sde->fbd", d_up_parts, up_low, preferred_element_type=jnp.float32)
    second_pull = jax.vjp(modulate, midway, shift_mlp, scale_mlp)[1]
    d_midway, d_shift_mlp, d_scale_mlp = second_pull(d_norm_two)
    d_midway = d_midway + upstream
    d_gate_attn = jnp.sum(d_midway * branch, axis=1, keepdims=True)
    d_branch = (d_midway * gate_attn).astype(low)
    grad_out = jnp.einsum("fbd,fbe->de", attended, d_branch, preferred_element_type=jnp.float32)
    grad_out_bias = token_sum(d_branch)
    d_attended = jnp.einsum("fbe,de->fbd", d_branch, out_low, preferred_element_type=jnp.float32)
    d_attended = d_attended.astype(low).reshape(head_shape)
    scores = attention_scores(query_heads, key_heads, valid_slots, score_scale)
    soft = jnp.exp(scores - log_total)
    d_soft = jnp.einsum(
        "fqhs,fkhs->fhqk", d_attended, value_heads, preferred_element_type=jnp.float32
    )
    d_value_heads = jnp.einsum(
        "fhqk,fqhs->fkhs", attention, d_attended, preferred_element_type=jnp.float32
    )
    d_scores = (soft * (d_soft - jnp.sum(soft * d_soft, axis=-1, keepdims=True))).astype(low)
    d_query_heads = (
        jnp.einsum("fhqk,fkhs->fqhs", d_scores, key_heads, preferred_element_type=jnp.float32)
        * score_scale
    )
    d_key_heads = (
        jnp.einsum("fhqk,fqhs->fkhs", d_scores, query_heads, preferred_element_type=jnp.float32)
        * score_scale
    )
    flat_shape = (frame_count, frame_len, model_width)
    d_query = d_query_heads.reshape(flat_shape).astype(low)
    d_key = d_key_heads.reshape(flat_shape).astype(low)
    d_value = d_value_heads.reshape(flat_shape).astype(low)
    grad_query, grad_key, grad_value = (
        jnp.einsum("fbd,fbe->de", norm_one, member, preferred_element_type=jnp.float32)
        for member in (d_query, d_key, d_value)
    )
    grad_query_bias = token_sum(d_query)
    grad_value_bias = token_sum(d_value)
    d_norm_one = sum(
        jnp.einsum("fbe,de->fbd", member, weight, preferred_element_type=jnp.float32)
        for member, weight in ((d_query, query_low), (d_key, key_low), (d_value, value_low))
    )
    first_pull = jax.vjp(modulate, frames_f, shift_attn, scale_attn)[1]
    d_frames, d_shift_attn, d_scale_attn = first_pull(d_norm_one)
    frames_grad = (d_frames + d_midway).astype(low)
    d_modulation = jnp.concatenate(
        [d_shift_attn, d_scale_attn, d_gate_attn, d_shift_mlp, d_scale_mlp, d_gate_mlp], axis=-1
    )[:, 0, :].astype(low)
    grad_mod_bias = d_modulation[0].astype(jnp.float32)
    grad_bias = jnp.concatenate(
        [
            grad_mod_bias,
            grad_query_bias,
            grad_value_bias,
            grad_out_bias,
            grad_up_bias,
            grad_down_bias,
        ]
    )
    terms = exchange(
        jnp.concatenate(
            [
                jnp.broadcast_to(d_modulation, (count, d_modulation.shape[1])),
                grad_bias.reshape(count, -1).astype(low),
            ],
            axis=1,
        )
    )
    d_mod_all, bias_terms = terms[:, : d_modulation.shape[1]], terms[:, d_modulation.shape[1] :]

    def grouped(member, group_rows):
        member = member.astype(low).reshape(4, count // 4, 4 * rows, model_width)
        return jnp.pad(member, ((0, 0), (0, 0), (0, group_rows - 4 * rows), (0, 0)))

    group_rows = -(-4 * rows // 16) * 16
    tall_group = -(-tall_rows // 16) * 16
    a_sum, b_sum, c_sum = reduce(
        grouped(jnp.stack([grad_query, grad_key, grad_value, grad_out]), group_rows),
        grouped(grad_up, group_rows),
        jnp.pad(
            grad_down.astype(low).reshape(count // 4, 4, tall_rows, model_width),
            ((0, 0), (0, 0), (0, tall_group - tall_rows), (0, 0)),
        ),
        rows,
        (True, False, False),
    )
    red_mod = lax.dot_general(
        silu_rows, d_mod_all, (((0,), (0,)), ((), ())), preferred_element_type=jnp.float32
    )
    a_sum = a_sum.astype(jnp.float32)
    red_qkv = a_sum[:3].transpose(1, 0, 2).reshape(rows, 3 * model_width)
    red_out = a_sum[3]
    red_up = b_sum.astype(jnp.float32).transpose(1, 0, 2).reshape(rows, hidden_width)
    red_down = c_sum[:tall_rows]
    red_bias = jnp.sum(bias_terms.astype(jnp.float32), axis=0)
    d_silu = lax.dot_general(
        d_mod_all, mod_low, (((1,), (1,)), ((), ())), preferred_element_type=jnp.float32
    )
    reduced = (red_mod, red_qkv, red_out, red_up, red_down, red_bias)
    partial_sq = sum((jnp.sum(member * member) for member in reduced))
    last = exchange(
        jnp.concatenate([d_silu, jnp.broadcast_to(partial_sq, (count, 1))], axis=1)
    )
    total_sq = jnp.sum(last[:, rows])
    silu_pull = jax.vjp(silu_act, cond_f)[1]
    cond_grad = silu_pull(last[:, :rows].reshape(1, model_width))[0]
    grad_norm = jnp.sqrt(total_sq)
    factor = jnp.minimum(1.0, CLIP / (grad_norm + 1e-06))
    clipped = tuple((member * factor for member in reduced))
    masters = (mod_weight, qkv_weight, out_weight, up_weight, down_weight, biases)
    states = (mod_state, qkv_state, out_state, up_state, down_state, bias_state)
    updated = [adam_update(masters[index], states[index], clipped[index]) for index in range(6)]
    return (
        (block_out, frames_grad, cond_grad, grad_norm)
        + clipped
        + tuple(pair[0] for pair in updated)
        + tuple(pair[1] for pair in updated)
    )


def solution(mesh):
    tokens = P(AXES, None, None)
    matrix = P(AXES, None)
    vector = P(AXES)
    state = P(None, AXES, None)
    weights = (matrix,) * 5 + (vector,)
    states = (state,) * 5 + (P(None, AXES),)
    return jax.shard_map(
        shards,
        mesh=mesh,
        in_specs=(tokens, matrix, matrix, tokens) + weights + states,
        out_specs=(tokens, tokens, matrix, P()) + weights + weights + states,
        check_vma=False,
    )
```

time: 1860 us -> 532 us (0.29)
  waiting for transfers between devices: 1390 us -> 21.6 us
  Pallas kernels: 0 us -> 267 us
  blocking collectives: 95.1 us -> 0 us
  other arithmetic: 84.9 us -> 51.2 us
  local copies, waits for them, and re-layouts: 102 us -> 71.6 us
  matrix products: 109 us -> 87 us
  starting transfers between devices: 40.1 us -> 19 us
    all_to_all x6 -> x4, waiting for transfers between devices: 1070 us -> 21.6 us  [exchange(): lax.all_to_all(packets, AXES, split_axis=0, concat_axis=0, tiled=True)]
    all_gather x5 -> x0, waiting for transfers between devices: 319 us -> none  [the longest x1 107 us: shards(): lax.all_gather(mod_weight.astype(jnp.bfloat16), ('wide', 'narrow'), axis=...]
    pallas_call x0 -> x2, Pallas kernels: none -> 267 us  [the longest x1 142 us: reduce(): pl.pallas_call(functools.partial(reduce_kernel, bits, rows, lates), out_s...]
    psum x1 -> x0, blocking collectives: 52.7 us -> none  [shards(): total_sq = lax.psum(partial_sq, ('wide', 'narrow'))]
    unnamed x181 -> x214, local copies, waits for them, and re-layouts: 75.7 us -> 28.9 us
    unnamed x1 -> x0, blocking collectives: 42.4 us -> none
    reduce_sum x6 -> x3, other arithmetic: 37.6 us -> 2.37 us  [the longest x1 1.68 us: shards(): modulation = jnp.sum(mod_terms, axis=0, keepdims=True) + mod_bias]
    dot_general x11 -> x18, matrix products: 76.6 us -> 55.2 us  [the longest x5 19.1 us: project(): jnp.einsum('fbd,de->fbe', values, weight, preferred_element_type=jnp.floa...]
  transfers between devices with their start and end apart: 11 -> 4, of which waited for: 11 -> 2; matrix products, arithmetic and copies ran while one was open for 8% -> 10% of each run, Pallas kernels for 0% -> 51%
where the time goes in v1:
time: 532 us; the launch traced here: 526 us
  Pallas kernels  267 us (50%)
  matrix products  87 us (16%)
  local copies, waits for them, and re-layouts  71.6 us (13%)
  other arithmetic  51.2 us (10%)
  waiting for transfers between devices  21.6 us (4%)
  starting transfers between devices  19 us (4%)
  between operations  9.14 us (2%)
    pallas_call x1, Pallas kernels, reduce(): pl.pallas_call(functools.partial(reduce_kernel, bits, rows, lates), out_s...  142 us
    pallas_call x1, Pallas kernels, gather(): pl.pallas_call(functools.partial(gather_kernel, bits, rows, lates), out_s...  125 us
    unnamed x214, local copies, waits for them, and re-layouts  28.9 us
    all_to_all x4, waiting for transfers between devices, exchange(): lax.all_to_all(packets, AXES, split_axis=0, concat_axis=0, tiled=True)  21.6 us
    dot_general x5, matrix products, project(): jnp.einsum('fbd,de->fbe', values, weight, preferred_element_type=jnp.floa...  19.1 us
    all_to_all x4, starting transfers between devices, exchange(): lax.all_to_all(packets, AXES, split_axis=0, concat_axis=0, tiled=True)  19 us
    another operation x13, other arithmetic, adam_update(): return (new_weight, jnp.stack([first, second, average]))  17.7 us
    reshape x1, local copies, waits for them, and re-layouts, shards(): up_low = b_all[:, :, :4 * rows].reshape(4, model_width, model_width)  15.5 us
  transfers between devices with their start and end apart: 4, of which 2 were waited for; matrix products, arithmetic and copies ran while one was open for 10% of the time, Pallas kernels for 51%

profile of v1, /device:TPU:0, one launch (start us, length us, event | category | flops | bytes accessed | tf_op | source)
XLA Modules:
  0.0 526.0 jit_solution(3096339305858820240)
XLA Ops:
  5.0 7.3 %all-to-all-start = ((bf16[32,2,270]{2,1,0:T(2,128)(2,1)}), bf16[32,2,270]{2,1,0:T(2,128)(2,1)S(1)}, u32[]{:S(2)}, u32[]{:S(2)}) async-start(bf16[32,2,270]{2,1,0:T(2,128)(2,1)} %reshape.707), calls=%async_computation | async-start | bytes 98304 | tf_op jit(solution)/shard_map/all_to_all | solution.py:416
  18.1 124.8 %gather_weights.1 = (bf16[4,8,144,1152]{3,2,1,0:T(8,128)(2,1)}, bf16[4,8,144,1152]{3,2,1,0:T(8,128)(2,1)}, bf16[8,4,144,1152]{3,2,1,0:T(8,128)(2,1)}) custom-call(bf16[4,36,1152]{2,1,0:T(8,128)(2,1)} %get-tuple-element.116.a_src, bf16[4,36,1152]{2,1,0:T(8,128)(2,1)} %get-tuple-element.115.b_src, bf16[144,1152]{1,0:T(8,128)(2,1)} %convert_element_type.234.c_src), custom_call_target="tpu_custom_call" | custom-call | bytes 400000000 | tf_op jit(solution)/shard_map/gather_weights/pallas_call | solution.py:192
  142.9 15.5 %copy.113 = bf16[4,1152,1152]{1,2,0:T(8,128)(2,1)} copy(bf16[4,1152,1152]{2,1,0:T(8,128)(2,1)} %bitcast.304) | data formatting | bytes 21233664 | tf_op jit(solution)/shard_map/reshape | solution.py:454
  160.1 1.8 copy.106
  162.0 4.7 all-to-all-start.1
  166.7 7.3 %fusion.134 = (bf16[1,8,144,1152]{3,2,1,0:T(8,128)(2,1)}, bf16[1,8,144,1152]{3,2,1,0:T(8,128)(2,1)S(1)}, bf16[1,8,144,1152]{3,2,1,0:T(8,128)(2,1)}, bf16[1,8,144,1152]{3,2,1,0:T(8,128)(2,1)}) fusion(bf16[4,8,144,1152]{3,2,1,0:T(8,128)(2,1)} %get-tuple-element.28), kind=kLoop, calls=%fused_computation.267 | loop fusion | bytes 21233664 | tf_op jit(solution)/shard_map/slice | solution.py:456
  175.0 14.4 %all-to-all-done.1 = f32[32,1,6912]{2,1,0:T(1,128)} async-done(((f32[32,1,6912]{2,1,0:T(1,128)}), f32[32,1,6912]{2,1,0:T(1,128)}, u32[]{:S(2)}, u32[]{:S(2)}) %all-to-all-start.1) | async-done | bytes 884768 | tf_op jit(solution)/shard_map/all_to_all | solution.py:416
  191.2 3.6 fusion.14
  194.9 2.1 copy.110
  197.0 1.9 convolution_convert_fusion.7
  200.2 2.4 fusion.18
  210.0 2.1 fusion.133
  212.4 12.6 %convolution_add_fusion = f32[256,4608]{1,0:T(8,128)} fusion(bf16[4608,1152]{1,0:T(8,128)(2,1)} %bitcast.308, f32[4608]{0:T(1024)S(1)} %split.58, f32[1,256,1152]{2,1,0:T(8,128)S(1)} %get-tuple-element.69, f32[1152]{0:T(1024)S(1)} %get-tuple-element.41, f32[1152]{0:T(1024)S(1)} %get-tuple-element.42, f32[256]{0:T(256)S(1)} %fusion.117, ...), kind=kOutput, calls=%fused_computation.7 | convolution fusion | flops 2720563200 | bytes 16544768 | tf_op jit(solution)/shard_map/fbd,sde->fbse/dot_general | solution.py:505
  225.0 11.4 %fusion.137 = (bf16[4608]{0:T(1024)(128)(2,1)}, bf16[256,4608]{1,0:T(8,128)(2,1)}) fusion(f32[256,4608]{1,0:T(8,128)} %convolution_add_fusion, bf16[4608,1152]{1,0:T(8,128)(2,1)} %bitcast.358, f32[1152]{0:T(1024)S(1)} %get-tuple-element.40, f32[256]{0:T(256)S(1)} %get-tuple-element.118, bf16[1,256,1152]{2,1,0:T(8,128)(2,1)S(1)} %copy-done.57), kind=kOutput, calls=%fused_computation.270 | convolution fusion | flops 2748575232 | bytes 18299392 | tf_op jit(solution)/shard_map/fbd,ed->fbe/dot_general | solution.py:518
  236.4 6.6 %fusion.35 = (bf16[1152]{0:T(1024)(128)(2,1)}, f32[256]{0:T(256)S(1)}, f32[256,1152,1]{1,0,2:T(8,128)}) fusion(f32[1,256,1152]{2,1,0:T(8,128)S(1)} %get-tuple-element.69, f32[256]{0:T(256)S(1)} %fusion.117, f32[256]{0:T(256)S(1)} %broadcast_multiply_fusion.3, f32[1152]{0:T(1024)S(1)} %get-tuple-element.42, bf16[4,1152,1152]{2,1,0:T(8,128)(2,1)S(1)} %bitcast.307, ...), kind=kOutput, calls=%fused_computation.79 | convolution fusion | flops 2719972096 | bytes 15345408 | tf_op jit(solution)/shard_map/fbse,sde->fbd/dot_general | solution.py:524
  247.7 1.9 convolution_convert_fusion.6
  249.5 2.1 copy.115
  251.6 4.2 multiply_reduce_fusion
  262.1 7.1 %convolution_convert_fusion.1 = bf16[4608,1152]{1,0:T(8,128)(2,1)} fusion(bf16[1,256,1152]{2,1,0:T(8,128)(2,1)S(1)} %copy-done.59, f32[1152]{0:T(1024)S(1)} %get-tuple-element.40, f32[256]{0:T(256)S(1)} %get-tuple-element.118, f32[256,4608]{1,0:T(8,128)S(1)} %bitcast.361), kind=kOutput, calls=%fused_computation.1 | convolution fusion | flops 2735013888 | bytes 15930880 | tf_op jit(solution)/shard_map/fbe,fbd->ed/dot_general | solution.py:516
  278.2 10.4 %fusion.34 = (bf16[1152]{0:T(1024)(128)(2,1)S(1)}, bf16[1152]{0:T(1024)(128)(2,1)S(1)}, bf16[1,256,1152]{2,1,0:T(8,128)(2,1)}, bf16[1,256,1152]{2,1,0:T(8,128)(2,1)}, bf16[1152,256]{0,1:T(8,128)(2,1)}) fusion(bf16[1,256,1152]{2,1,0:T(8,128)(2,1)S(1)} %copy-done.60, f32[256]{0:T(256)S(1)} %copy-done.88, f32[256,1152]{1,0:T(8,128)} %get-tuple-element.101, ...), kind=kOutput, calls=%fused_computation.77 | convolution fusion | flops 2736486400 | bytes 23032320 | tf_op jit(solution)/shard_map/fbd,de->fbe/dot_general | solution.py:486
  305.4 4.0 all-to-all-start.2
  309.5 2.4 fusion.12
  317.1 5.1 pad_maximum_fusion.a_in
  322.3 5.9 %convolution_convert_fusion = bf16[4,1152,1152]{1,2,0:T(8,128)(2,1)} fusion(bf16[32,4,8,1152]{3,2,1,0:T(8,128)(2,1)S(1)} %bitcast.317, f32[1,256,1152]{2,1,0:T(8,128)S(1)} %get-tuple-element.69, f32[1152]{0:T(1024)S(1)} %copy-done.63, f32[1152]{0:T(1024)S(1)} %get-tuple-element.42, f32[256]{0:T(256)S(1)} %copy-done.80, f32[256]{0:T(256)S(1)} %copy-done.73), kind=kOutput, calls=%fused_computation | convolution fusion | flops 2724691968 | bytes 14167040 | tf_op jit(solution)/shard_map/fbd,fbse->sde/dot_general | solution.py:522
  328.2 141.7 %reduce_gradients.1 = (bf16[4,36,1152]{2,1,0:T(8,128)(2,1)}, bf16[4,36,1152]{2,1,0:T(8,128)(2,1)}, f32[144,1152]{1,0:T(8,128)}) custom-call(bf16[4,8,144,1152]{3,2,1,0:T(8,128)(2,1)} %pad_maximum_fusion.a_in, bf16[4,8,144,1152]{3,2,1,0:T(8,128)(2,1)} %bitcast.303, bf16[8,4,144,1152]{3,2,1,0:T(8,128)(2,1)} %bitcast.309), custom_call_target="tpu_custom_call" | custom-call | bytes 400000000 | tf_op jit(solution)/shard_map/reduce_gradients/pallas_call | solution.py:331
  471.7 1.8 fusion.42
  476.1 2.7 multiply_reduce_fusion.2
  483.9 3.0 all-to-all-start.3
  486.9 7.2 %all-to-all-done.3 = f32[32,1,37]{2,1,0:T(1,128)S(1)} async-done(((f32[32,1,37]{2,1,0:T(1,128)}), f32[32,1,37]{2,1,0:T(1,128)S(1)}, u32[]{:S(2)}, u32[]{:S(2)}) %all-to-all-start.3) | async-done | bytes 4768 | tf_op jit(solution)/shard_map/all_to_all | solution.py:416
  497.8 2.1 fusion.98
  506.4 1.9 fusion.41
  517.0 1.9 pad_maximum_fusion.1
  (321 shorter events, 92.8 us)
Async XLA Ops:
  0.7 14.2 %copy-start.53 = (f32[36,1152]{1,0:T(8,128)S(1)}, f32[36,1152]{1,0:T(8,128)}, u32[]{:S(2)}) copy-start(f32[36,1152]{1,0:T(8,128)} %param.22) | copy-start | bytes 497668
  0.7 14.3 %copy-start.48 = (f32[36,3456]{1,0:T(8,128)S(1)}, f32[36,3456]{1,0:T(8,128)}, u32[]{:S(2)}) copy-start(f32[36,3456]{1,0:T(8,128)} %param.21) | copy-start | bytes 1492996
  5.0 154.7 %all-to-all-start = ((bf16[32,2,270]{2,1,0:T(2,128)(2,1)}), bf16[32,2,270]{2,1,0:T(2,128)(2,1)S(1)}, u32[]{:S(2)}, u32[]{:S(2)}) async-start(bf16[32,2,270]{2,1,0:T(2,128)(2,1)} %reshape.707), calls=%async_computation | async-start | bytes 98304 | tf_op jit(solution)/shard_map/all_to_all | solution.py:416
  16.8 255.3 %copy-start.70 = (f32[256]{0:T(256)}, f32[256]{0:T(256)S(1)}, u32[]{:S(2)}) copy-start(f32[256]{0:T(256)S(1)} %broadcast_multiply_fusion.4) | copy-start | bytes 3076
  17.1 149.6 %copy-start.77 = (f32[256]{0:T(256)}, f32[256]{0:T(256)S(1)}, u32[]{:S(2)}) copy-start(f32[256]{0:T(256)S(1)} %fusion.32) | copy-start | bytes 3076
  142.9 17.0 %copy-start.11 = (f32[36,6912]{1,0:T(8,128)S(1)}, f32[36,6912]{1,0:T(8,128)}, u32[]{:S(2)}) copy-start(f32[36,6912]{1,0:T(8,128)} %param.20) | copy-start | bytes 2985988
  159.7 102.3 %copy-start.87 = (f32[256]{0:T(256)}, f32[256]{0:T(256)S(1)}, u32[]{:S(2)}) copy-start(f32[256]{0:T(256)S(1)} %get-tuple-element.118) | copy-start | bytes 3076
  159.9 14.1 %copy-start.61 = (bf16[32,1,540]{2,0,1:T(8,128)(2,1)}, bf16[32,1,540]{2,0,1:T(8,128)(2,1)S(1)}, u32[]{:S(2)}) copy-start(bf16[32,1,540]{2,0,1:T(8,128)(2,1)S(1)} %copy.163) | copy-start | bytes 103684
  162.0 27.4 %all-to-all-start.1 = ((f32[32,1,6912]{2,1,0:T(1,128)}), f32[32,1,6912]{2,1,0:T(1,128)}, u32[]{:S(2)}, u32[]{:S(2)}) async-start(f32[32,1,6912]{2,1,0:T(1,128)} %copy.106), calls=%async_computation.1 | async-start | bytes 1769472 | tf_op jit(solution)/shard_map/all_to_all | solution.py:416
  166.7 38.9 %copy-start.75 = (f32[256]{0:T(256)}, f32[256]{0:T(256)S(1)}, u32[]{:S(2)}) copy-start(f32[256]{0:T(256)S(1)} %fusion.116) | copy-start | bytes 3076
  174.0 23.0 %copy-start.8 = (bf16[1,8,144,1152]{3,2,1,0:T(8,128)(2,1)}, bf16[1,8,144,1152]{3,2,1,0:T(8,128)(2,1)S(1)}, u32[]{:S(2)}) copy-start(bf16[1,8,144,1152]{3,2,1,0:T(8,128)(2,1)S(1)} %get-tuple-element.73) | copy-start | bytes 7962628
  191.2 14.4 %copy-start.81 = (f32[1152]{0:T(1024)}, f32[1152]{0:T(1024)S(1)}, u32[]{:S(2)}) copy-start(f32[1152]{0:T(1024)S(1)} %get-tuple-element.43) | copy-start | bytes 13828
  191.2 21.1 %copy-start.62 = (f32[1152]{0:T(1024)}, f32[1152]{0:T(1024)S(1)}, u32[]{:S(2)}) copy-start(f32[1152]{0:T(1024)S(1)} %get-tuple-element.41) | copy-start | bytes 13828
  191.2 70.8 %copy-start.64 = (f32[1152]{0:T(1024)}, f32[1152]{0:T(1024)S(1)}, u32[]{:S(2)}) copy-start(f32[1152]{0:T(1024)S(1)} %get-tuple-element.40) | copy-start | bytes 13828
  212.1 31.0 %copy-start.72 = (f32[256]{0:T(256)}, f32[256]{0:T(256)S(1)}, u32[]{:S(2)}) copy-start(f32[256]{0:T(256)S(1)} %broadcast_multiply_fusion.3) | copy-start | bytes 3076
  212.3 30.7 %copy-start.79 = (f32[256]{0:T(256)}, f32[256]{0:T(256)S(1)}, u32[]{:S(2)}) copy-start(f32[256]{0:T(256)S(1)} %fusion.117) | copy-start | bytes 3076
  212.4 12.6 %copy-start.57 = (bf16[1,256,1152]{2,1,0:T(8,128)(2,1)S(1)}, bf16[1,256,1152]{2,1,0:T(8,128)(2,1)}, u32[]{:S(2)}) copy-start(bf16[1,256,1152]{2,1,0:T(8,128)(2,1)} %param.19) | copy-start | bytes 1769476
  212.4 24.0 %slice-start = ((s8[10616832]{0:T(1024)(128)(4,1)}), s8[4194304]{0:T(1024)(128)(4,1)S(1)}, s32[]{:S(2)}) async-start(s8[10616832]{0:T(1024)(128)(4,1)} %bitcast.305), calls=%async_computation.4 | async-start | bytes 8388608
  225.0 11.4 %slice-start.1 = ((s8[10616832]{0:T(1024)(128)(4,1)}), s8[4194304]{0:T(1024)(128)(4,1)S(1)}, s32[]{:S(2)}) async-start(s8[10616832]{0:T(1024)(128)(4,1)} %bitcast.305), calls=%async_computation.5 | async-start | bytes 8388608
  225.0 11.4 %slice-start.2 = ((s8[10616832]{0:T(1024)(128)(4,1)}), s8[2228224]{0:T(1024)(128)(4,1)S(1)}, s32[]{:S(2)}) async-start(s8[10616832]{0:T(1024)(128)(4,1)} %bitcast.305), calls=%async_computation.6 | async-start | bytes 4456448
  251.6 10.4 %slice-start.3 = ((s8[4718592]{0:T(1024)(128)(4,1)}), s8[4194304]{0:T(1024)(128)(4,1)S(1)}, s32[]{:S(2)}) async-start(s8[4718592]{0:T(1024)(128)(4,1)} %bitcast.360), calls=%async_computation.7 | async-start | bytes 8388608
  258.5 10.7 %copy-start.43 = (bf16[16,72,256]{2,1,0:T(8,128)(2,1)}, bf16[16,72,256]{2,1,0:T(8,128)(2,1)S(1)}, u32[]{:S(2)}) copy-start(bf16[16,72,256]{2,1,0:T(8,128)(2,1)S(1)} %get-tuple-element.108) | copy-start | bytes 1769476
  259.8 10.5 %copy-start.23 = (bf16[16,72,256]{2,1,0:T(8,128)(2,1)}, bf16[16,72,256]{2,1,0:T(8,128)(2,1)S(1)}, u32[]{:S(2)}) copy-start(bf16[16,72,256]{2,1,0:T(8,128)(2,1)S(1)} %fusion.28) | copy-start | bytes 1769476
  261.3 10.8 %copy-start.25 = (bf16[16,72,256]{2,1,0:T(8,128)(2,1)}, bf16[16,72,256]{2,1,0:T(8,128)(2,1)S(1)}, u32[]{:S(2)}) copy-start(bf16[16,72,256]{2,1,0:T(8,128)(2,1)S(1)} %get-tuple-element.110) | copy-start | bytes 1769476
  278.2 11.1 %copy-start.68 = (bf16[1152]{0:T(1024)(128)(2,1)S(1)}, bf16[1152]{0:T(1024)(128)(2,1)}, u32[]{:S(2)}) copy-start(bf16[1152]{0:T(1024)(128)(2,1)} %bitcast_reduce_fusion) | copy-start | bytes 6916
  278.2 11.6 %copy-start.91 = (bf16[1152]{0:T(1024)(128)(2,1)S(1)}, bf16[1152]{0:T(1024)(128)(2,1)}, u32[]{:S(2)}) copy-start(bf16[1152]{0:T(1024)(128)(2,1)} %get-tuple-element.34) | copy-start | bytes 6916
  305.4 169.5 %all-to-all-start.2 = ((bf16[32,2,3708]{2,1,0:T(2,128)(2,1)}), bf16[32,2,3708]{2,1,0:T(2,128)(2,1)S(1)}, u32[]{:S(2)}, u32[]{:S(2)}) async-start(bf16[32,2,3708]{2,1,0:T(2,128)(2,1)} %reshape.709), calls=%async_computation.2 | async-start | bytes 950272 | tf_op jit(solution)/shard_map/all_to_all | solution.py:416
  475.8 11.1 %copy-start.74 = (f32[3,504]{1,0:T(4,128)S(1)}, f32[3,504]{1,0:T(4,128)}, u32[]{:S(2)}) copy-start(f32[3,504]{1,0:T(4,128)} %param.31) | copy-start | bytes 18148
  476.1 19.5 %copy-start.52 = (bf16[4,36,1152]{2,1,0:T(8,128)(2,1)S(1)}, bf16[4,36,1152]{2,1,0:T(8,128)(2,1)}, u32[]{:S(2)}) copy-start(bf16[4,36,1152]{2,1,0:T(8,128)(2,1)} %get-tuple-element.32) | copy-start | bytes 995332
  483.9 10.2 %all-to-all-start.3 = ((f32[32,1,37]{2,1,0:T(1,128)}), f32[32,1,37]{2,1,0:T(1,128)S(1)}, u32[]{:S(2)}, u32[]{:S(2)}) async-start(f32[32,1,37]{2,1,0:T(1,128)} %bitcast.70), calls=%async_computation.3 | async-start | bytes 32768 | tf_op jit(solution)/shard_map/all_to_all | solution.py:416
  502.3 8.0 %copy-start.47 = (f32[5,8,3,1152]{3,1,2,0:T(8,128)}, f32[5,8,3,1152]{3,1,2,0:T(8,128)S(1)}, u32[]{:S(2)}) copy-start(f32[5,8,3,1152]{3,1,2,0:T(8,128)S(1)} %copy.146) | copy-start | bytes 1658884
  503.6 8.5 %copy-start.35 = (f32[5,8,4,1152]{3,1,2,0:T(8,128)}, f32[5,8,4,1152]{3,1,2,0:T(8,128)S(1)}, u32[]{:S(2)}) copy-start(f32[5,8,4,1152]{3,1,2,0:T(8,128)S(1)} %copy.147) | copy-start | bytes 2211844
  (69 other events, 173.2 us)
